TPU v7x, 32 devices: a whole 2x2x4 slice. The times are simulated.
32 devices in a mesh: blk: 16 (over z, y, core), grp: 2 (over x).
Axes of the slice: x: 2, y: 2, z: 4, core: 2. Of those that a mesh axis runs over, the one named last changes fastest.
Arguments:
- images: float32 [4096, 768], P(('blk', 'grp')), may hold values from -0.24 to 0.24
- texts: float32 [4096, 768], P(('blk', 'grp')), may hold values from -0.24 to 0.24
- log_temp: float32 [1], replicated, may hold values from 2.3 to 3
- bias: float32 [1], replicated, may hold values from -3 to -1
- row_weight: float32 [4096], P(('blk', 'grp')), may hold values from 0.5 to 2
Outputs:
- row_loss: float32 [4096], P(('blk', 'grp'))
- grad_images: float32 [4096, 768], P(('blk', 'grp'))
- grad_texts: float32 [4096, 768], P(('blk', 'grp'))
All inputs are finite; a program needn't handle non-finite values.
Results may differ from a plain program's by a relative error of at most 0.00013.
Values sent between devices are 32-bit elements; how exact they have to be, the bound alone decides.
No kernel may reach another device: no remote copies, remote signals or barrier semaphores. Data moves between devices by JAX's collectives and lax.ppermute only.
A program may use at most 64 MiB of HBM per device.

v0:
```python
import jax
import jax.numpy as jnp
from jax import lax
from jax.sharding import PartitionSpec as P

REACH = 1


def passed_along(x, axis, by):
    length = lax.axis_size(axis)
    return lax.ppermute(x, axis, [(i, (i + by) % length) for i in range(length)])


def normed(values):
    scale = lax.rsqrt(jnp.sum(values * values, axis=1, keepdims=True) + 1e-06)
    return (values * scale, scale)


def unnormed(grad, unit, scale):
    return scale * (grad - unit * jnp.sum(unit * grad, axis=1, keepdims=True))


def tile_terms(left, right, temper, offset_b, weight, positive):
    logits = (
        temper * jnp.einsum("id,jd->ij", left, right, precision=lax.Precision.HIGHEST) + offset_b
    )
    labels = jnp.where(positive, 1.0, -1.0)
    losses = jax.nn.softplus(-labels * logits)
    slope = -labels * jax.nn.sigmoid(-labels * logits) * weight[:, None]
    return (jnp.sum(losses, axis=1), slope)


def shards(images, texts, log_temp, bias, row_weight):
    unit_x, scale_x = normed(images)
    unit_y, scale_y = normed(texts)
    temper = jnp.exp(log_temp[0])
    offset_b = bias[0]
    count = images.shape[0]
    members = lax.axis_size("grp")
    group = count * members
    mine = lax.axis_index("grp")
    group_x, group_w = (
        lax.all_gather(unit_x, "grp", axis=0, tiled=True),
        lax.all_gather(row_weight, "grp", axis=0, tiled=True),
    )
    window = {0: unit_y}
    current = unit_y
    step = 1
    current = passed_along(current, "blk", -1)
    window[step] = current
    current = unit_y
    step = 1
    current = passed_along(current, "blk", 1)
    window[-step] = current
    rows = lax.broadcasted_iota(jnp.int32, (group, count), 0)
    cols = lax.broadcasted_iota(jnp.int32, (group, count), 1)
    diagonal = rows == mine * count + cols
    nothing = jnp.zeros((group, count), bool)
    grad_group = jnp.zeros_like(group_x)
    group_sums = jnp.zeros((group,), jnp.float32)
    text_terms = {}
    for offset in range(-REACH, REACH + 1):
        positive = diagonal if offset == 0 else nothing
        part_sums, slope = tile_terms(group_x, window[offset], temper, offset_b, group_w, positive)
        group_sums = group_sums + part_sums
        grad_group = grad_group + temper * jnp.dot(
            slope, window[offset], precision=lax.Precision.HIGHEST
        )
        text_terms[offset] = temper * jnp.einsum(
            "ij,id->jd", slope, group_x, precision=lax.Precision.HIGHEST
        )
    step = 1
    carried = passed_along(text_terms[step], "blk", 1)
    step = 1
    returned = passed_along(text_terms[-step], "blk", -1)
    grad_y = text_terms[0] + carried + returned
    grad_x, sums = (
        lax.psum_scatter(grad_group, "grp", scatter_dimension=0, tiled=True),
        lax.psum_scatter(group_sums, "grp", scatter_dimension=0, tiled=True),
    )
    row_loss = sums / ((2 * REACH + 1) * group)
    return (row_loss, unnormed(grad_x, unit_x, scale_x), unnormed(grad_y, unit_y, scale_y))


def solution(mesh):
    placed = (P(("blk", "grp"), None), P(("blk", "grp"), None), P(), P(), P(("blk", "grp")))
    return jax.shard_map(
        shards,
        mesh=mesh,
        in_specs=placed,
        out_specs=(P(("blk", "grp")), P(("blk", "grp"), None), P(("blk", "grp"), None)),
        check_vma=False,
    )
```

profile of v0, /device:TPU:0, one launch (start us, length us, event | category | flops | bytes accessed | tf_op | source)
XLA Modules:
  0.0 63.5 jit_solution(8459419432554972889)
XLA Ops:
  7.2 1.1 %multiply_reduce_fusion.2 = f32[128]{0:T(128)S(1)} fusion(f32[128,768]{1,0:T(8,128)} %param.6), kind=kLoop, calls=%fused_computation.19 | loop fusion | flops 196480 | bytes 393728 | tf_op jit(solution)/shard_map/reduce_sum | solution.py:15
  8.5 5.5 %collective-permute-start.1 = (f32[128,768]{1,0:T(8,128)S(1)}, f32[128,768]{1,0:T(8,128)S(1)}, u32[]{:S(2)}, u32[]{:S(2)}) collective-permute-start(f32[128,768]{1,0:T(8,128)S(1)} %broadcast_multiply_fusion), channel_id=1, source_target_pairs={{0,30},{2,0},{4,2},{6,4},{8,6},{10,8},{12,10},{14,12},{16,14},{18,... | collective-permute-start | bytes 1179656 | tf_op jit(solution)/shard_map/ppermute | solution.py:11
  14.9 9.4 %all_gather.6 = f32[256,768]{1,0:T(8,128)S(1)} all-gather(f32[128,768]{1,0:T(8,128)S(1)} %broadcast_multiply_fusion.1), channel_id=1, replica_groups=mesh['blk'=16,'grp'=2] {'grp'}, dimensions={0}, use_global_device_ids=true | all-gather | bytes 1179648 | tf_op jit(solution)/shard_map/all_gather | solution.py:43
  25.0 0.6 %copy-done.3 = f32[128]{0:T(128)S(1)} copy-done((f32[128]{0:T(128)S(1)}, f32[128]{0:T(128)}, u32[]{:S(2)}) %copy-start.3) | copy-done | bytes 536
  25.7 4.2 %all-gather = f32[2,1,128]{2,1,0:T(1,128)S(1)} all-gather(f32[1,1,128]{2,1,0:T(1,128)S(1)} %bitcast.26), channel_id=1, replica_groups=mesh['blk'=16,'grp'=2] {'grp'}, dimensions={0}, use_global_device_ids=true | all-gather | bytes 1536 | tf_op jit(solution)/shard_map/all_gather | solution.py:44
  29.9 1.0 %fusion.9 = (f32[256]{0:T(256)S(1)}, f32[256,128]{0,1:T(8,128)S(1)}) fusion(f32[]{:T(128)} %bitcast.19, f32[256,768]{1,0:T(8,128)S(1)} %all_gather.6, f32[128,768]{1,0:T(8,128)S(1)} %broadcast_multiply_fusion, f32[]{:T(128)} %bitcast, s32[128]{0:T(128)S(1)} %iota_add_fusion), kind=kOutput, calls=%fused_computation.27 | convolution fusion | flops 302415616 | bytes 1312264 | tf_op jit(solution)/shard_map/id,jd->ij/dot_general | solution.py:25
  30.9 0.9 %fusion.16 = f32[256,768]{1,0:T(8,128)S(1)} fusion(f32[128,768]{1,0:T(8,128)S(1)} %broadcast_multiply_fusion, f32[256,128]{0,1:T(8,128)S(1)} %get-tuple-element.8, f32[256]{0:T(256)S(1)} %bitcast.20, s32[128]{0:T(128)S(1)} %iota_add_fusion), kind=kOutput, calls=%fused_computation.44 | convolution fusion | flops 302252032 | bytes 1312256 | tf_op jit(solution)/shard_map/dot_general | solution.py:66
  31.8 1.0 %fusion.10 = (f32[256]{0:T(256)S(1)}, f32[256,128]{0,1:T(8,128)S(1)}) fusion(f32[]{:T(128)} %bitcast.18, f32[256,768]{1,0:T(8,128)S(1)} %all_gather.6, f32[128,768]{1,0:T(8,128)S(1)} %collective-permute-done.1, f32[]{:T(128)} %bitcast), kind=kOutput, calls=%fused_computation.28 | convolution fusion | flops 302284544 | bytes 1311752 | tf_op jit(solution)/shard_map/id,jd->ij/dot_general | solution.py:25
  32.8 0.8 %fusion.11 = f32[256,768]{1,0:T(8,128)S(1)} fusion(f32[128,768]{1,0:T(8,128)S(1)} %collective-permute-done.1, f32[256,128]{0,1:T(8,128)S(1)} %get-tuple-element.4, f32[256]{0:T(256)S(1)} %bitcast.21), kind=kOutput, calls=%fused_computation.34 | convolution fusion | flops 302120960 | bytes 1311744 | tf_op jit(solution)/shard_map/dot_general | solution.py:66
  33.7 1.0 %fusion.8 = (f32[256]{0:T(256)S(1)}, f32[256,128]{0,1:T(8,128)S(1)}) fusion(f32[]{:T(128)} %bitcast.17, f32[256,768]{1,0:T(8,128)S(1)} %all_gather.6, f32[128,768]{1,0:T(8,128)S(1)} %collective-permute-done, f32[]{:T(128)} %bitcast), kind=kOutput, calls=%fused_computation.26 | convolution fusion | flops 302284544 | bytes 1311752 | tf_op jit(solution)/shard_map/id,jd->ij/dot_general | solution.py:25
  34.7 1.7 %fusion.1 = f32[256,768]{1,0:T(8,128)} fusion(f32[256,768]{1,0:T(8,128)S(1)} %fusion.11, f32[256,768]{1,0:T(8,128)S(1)} %fusion.16, f32[128,768]{1,0:T(8,128)S(1)} %collective-permute-done, f32[]{:T(128)} %bitcast, f32[256,128]{0,1:T(8,128)S(1)} %get-tuple-element.6, f32[256]{0:T(256)S(1)} %bitcast.22), kind=kOutput, calls=%fused_computation.2 | convolution fusion | flops 302710784 | bytes 2884612 | tf_op jit(solution)/shard_map/dot_general | solution.py:66
  36.4 1.3 %convolution_multiply_fusion = f32[128,768]{1,0:T(8,128)} fusion(f32[256,768]{1,0:T(8,128)S(1)} %all_gather.6, f32[]{:T(128)} %bitcast, f32[256,128]{0,1:T(8,128)S(1)} %get-tuple-element.6, f32[256]{0:T(256)S(1)} %bitcast.23), kind=kOutput, calls=%fused_computation.3 | convolution fusion | flops 302219264 | bytes 1311748 | tf_op jit(solution)/shard_map/ij,id->jd/dot_general | solution.py:69
  37.8 0.6 convolution_multiply_fusion.1
  38.4 2.7 %collective-permute-start.3 = (f32[128,768]{1,0:T(8,128)}, f32[128,768]{1,0:T(8,128)S(1)}, u32[]{:S(2)}, u32[]{:S(2)}) collective-permute-start(f32[128,768]{1,0:T(8,128)} %convolution_multiply_fusion), channel_id=1, source_target_pairs={{0,30},{2,0},{4,2},{6,4},{8,6},{10,8},{12,10},{14,12},{16,14},{18,... | collective-permute-start | bytes 1179656 | tf_op jit(solution)/shard_map/ppermute | solution.py:11
  41.0 0.7 %copy-done.4 = u32[32]{0:T(128)S(1)} copy-done((u32[32]{0:T(128)S(1)}, u32[32]{0:T(128)}, u32[]{:S(2)}) %copy-start.4) | copy-done | bytes 152
  41.7 0.6 dynamic-slice
  42.9 5.1 %all-reduce = f32[256]{0:T(256)S(1)} all-reduce(f32[256]{0:T(256)S(1)} %add_add_fusion), channel_id=2, replica_groups=mesh['blk'=16,'grp'=2] {'grp'}, use_global_device_ids=true, to_apply=%region_5.6.clone | all-reduce | flops 256 | bytes 2048
  48.1 0.6 dynamic-slice_multiply_fusion
  48.7 2.3 %collective-permute-done.2 = f32[128,768]{1,0:T(8,128)S(1)} collective-permute-done((f32[128,768]{1,0:T(8,128)S(1)}, f32[128,768]{1,0:T(8,128)S(1)}, u32[]{:S(2)}, u32[]{:S(2)}) %collective-permute-start.2) | collective-permute-done | bytes 393248 | tf_op jit(solution)/shard_map/ppermute | solution.py:11
  50.9 0.7 %multiply_reduce_fusion = (f32[128]{0:T(128)S(1)}, f32[128,768]{1,0:T(8,128)S(1)}) fusion(f32[128,768]{1,0:T(8,128)S(1)} %broadcast_multiply_fusion, f32[128,768]{1,0:T(8,128)S(1)} %collective-permute-done.3, f32[128,768]{1,0:T(8,128)S(1)} %collective-permute-done.2, f32[256,768]{1,0:T(8,128)S(1)} %all_gather.6, f32[256,128]{0,1:T(8,128)S(1)} %get-tuple-element.8, ...), kind=kOutput, calls=%fused_computation.16 | convolution fusion | flops 302743424 | bytes 2492420 | tf_op jit(solution)/shard_map/ij,id->jd/dot_general | solution.py:69
  51.6 0.9 %subtract_multiply_fusion = f32[128,768]{1,0:T(8,128)} fusion(f32[128,768]{1,0:T(8,128)S(1)} %get-tuple-element.10, f32[128]{0:T(128)S(1)} %get-tuple-element.9, f32[128]{0:T(128)S(1)} %add_rsqrt_fusion, f32[128,768]{1,0:T(8,128)S(1)} %copy-done.1), kind=kLoop, calls=%fused_computation.15 | loop fusion | flops 393216 | bytes 1180672 | tf_op jit(solution)/shard_map/mul | solution.py:20
  52.5 1.9 %reduce-scatter.2.cloned.1.call-done = f32[128,768]{1,0:T(8,128)} async-done(((f32[256,768]{1,0:T(8,128)}), f32[128,768]{1,0:T(8,128)}) %reduce-scatter.2.cloned.1.call-update) | async-done | bytes 393232 | tf_op jit(solution)/shard_map/reduce_scatter | solution.py:78
  54.5 1.2 %multiply_reduce_fusion.1 = f32[128]{0:T(128)S(1)} fusion(f32[128,768]{1,0:T(8,128)} %reduce-scatter.2.cloned.1.call-done, f32[128,768]{1,0:T(8,128)S(1)} %copy-done, f32[128]{0:T(128)S(1)} %add_rsqrt_fusion.1), kind=kLoop, calls=%fused_computation.18 | loop fusion | flops 294784 | bytes 787456 | tf_op jit(solution)/shard_map/reduce_sum | solution.py:20
  55.7 0.9 %subtract_multiply_fusion.1 = f32[128,768]{1,0:T(8,128)} fusion(f32[128,768]{1,0:T(8,128)S(1)} %copy-done.2, f32[128]{0:T(128)S(1)} %multiply_reduce_fusion.1, f32[128]{0:T(128)S(1)} %add_rsqrt_fusion.1, f32[128,768]{1,0:T(8,128)S(1)} %copy-done), kind=kLoop, calls=%fused_computation.17 | loop fusion | flops 393216 | bytes 1180672 | tf_op jit(solution)/shard_map/mul | solution.py:20
  (22 shorter events, 0.4 us)
Async XLA Ops:
  7.2 1.2 %copy-start.1 = (f32[128,768]{1,0:T(8,128)S(1)}, f32[128,768]{1,0:T(8,128)}, u32[]{:S(2)}) copy-start(f32[128,768]{1,0:T(8,128)} %param.6) | copy-start | bytes 1179652
  7.2 47.3 %reduce-scatter.2.cloned.1.call-start = ((), (), s32[]{:S(2)}) async-start(), calls=%async_computation.1 | async-start | bytes 1179648 | tf_op jit(solution)/shard_map/reduce_scatter | solution.py:78
  8.4 6.3 %copy-start = (f32[128,768]{1,0:T(8,128)S(1)}, f32[128,768]{1,0:T(8,128)}, u32[]{:S(2)}) copy-start(f32[128,768]{1,0:T(8,128)} %param.5) | copy-start | bytes 1179652
  8.5 23.3 %collective-permute-start.1 = (f32[128,768]{1,0:T(8,128)S(1)}, f32[128,768]{1,0:T(8,128)S(1)}, u32[]{:S(2)}, u32[]{:S(2)}) collective-permute-start(f32[128,768]{1,0:T(8,128)S(1)} %broadcast_multiply_fusion), channel_id=1, source_target_pairs={{0,30},{2,0},{4,2},{6,4},{8,6},{10,8},{12,10},{14,12},{16,14},{18,... | collective-permute-start | bytes 1179656 | tf_op jit(solution)/shard_map/ppermute | solution.py:11
  14.0 19.6 %collective-permute-start = (f32[128,768]{1,0:T(8,128)S(1)}, f32[128,768]{1,0:T(8,128)S(1)}, u32[]{:S(2)}, u32[]{:S(2)}) collective-permute-start(f32[128,768]{1,0:T(8,128)S(1)} %broadcast_multiply_fusion), channel_id=1, source_target_pairs={{0,2},{2,4},{4,6},{6,8},{8,10},{10,12},{12,14},{14,16},{16,18},{18... | collective-permute-start | bytes 1179656 | tf_op jit(solution)/shard_map/ppermute | solution.py:11
  25.0 0.7 %copy-start.3 = (f32[128]{0:T(128)S(1)}, f32[128]{0:T(128)}, u32[]{:S(2)}) copy-start(f32[128]{0:T(128)} %param.9) | copy-start | bytes 1540
  38.4 10.3 %collective-permute-start.3 = (f32[128,768]{1,0:T(8,128)}, f32[128,768]{1,0:T(8,128)S(1)}, u32[]{:S(2)}, u32[]{:S(2)}) collective-permute-start(f32[128,768]{1,0:T(8,128)} %convolution_multiply_fusion), channel_id=1, source_target_pairs={{0,30},{2,0},{4,2},{6,4},{8,6},{10,8},{12,10},{14,12},{16,14},{18,... | collective-permute-start | bytes 1179656 | tf_op jit(solution)/shard_map/ppermute | solution.py:11
  41.0 9.9 %collective-permute-start.2 = (f32[128,768]{1,0:T(8,128)S(1)}, f32[128,768]{1,0:T(8,128)S(1)}, u32[]{:S(2)}, u32[]{:S(2)}) collective-permute-start(f32[128,768]{1,0:T(8,128)S(1)} %convolution_multiply_fusion.1), channel_id=1, source_target_pairs={{0,2},{2,4},{4,6},{6,8},{8,10},{10,12},{12,14},{14,16},{16,18},{18... | collective-permute-start | bytes 1179656 | tf_op jit(solution)/shard_map/ppermute | solution.py:11
  41.0 0.7 %copy-start.4 = (u32[32]{0:T(128)S(1)}, u32[32]{0:T(128)}, u32[]{:S(2)}) copy-start(u32[32]{0:T(128)} %constant.26) | copy-start | bytes 388
  54.5 1.3 %copy-start.2 = (f32[128,768]{1,0:T(8,128)S(1)}, f32[128,768]{1,0:T(8,128)}, u32[]{:S(2)}) copy-start(f32[128,768]{1,0:T(8,128)} %reduce-scatter.2.cloned.1.call-done) | copy-start | bytes 1179652
Sparse Core Ops, SparseCore 0:
  36.5 17.8 reduce-scatter.1
where the time goes:
time: 63.7 us; the launch traced here: 63.5 us
  blocking collectives  18.7 us (29%)
  between operations  16.2 us (25%)
  matrix products  9.09 us (14%)
  starting transfers between devices  8.24 us (13%)
  other arithmetic  5.08 us (8%)
  waiting for transfers between devices  4.21 us (7%)
  local copies, waits for them, and re-layouts  1.9 us (3%)
    all_gather x1, blocking collectives, shards(): lax.all_gather(unit_x, 'grp', axis=0, tiled=True)  9.38 us
    ppermute x4, starting transfers between devices, passed_along(): lax.ppermute(x, axis, [(i, (i + by) % length) for i in range(length)])  8.2 us
    unnamed x1, blocking collectives  5.14 us
    all_gather x1, blocking collectives, shards(): lax.all_gather(row_weight, 'grp', axis=0, tiled=True)  4.22 us
    dot_general x3, matrix products, shards(): jnp.dot(slope, window[offset], precision=lax.Precision.HIGHEST)  3.45 us
    dot_general x3, matrix products, tile_terms(): jnp.einsum('id,jd->ij', left, right, precision=lax.Precision.HIGHEST)  3 us
    dot_general x3, matrix products, shards(): jnp.einsum('ij,id->jd', slope, group_x, precision=lax.Precision.HIGHEST)  2.65 us
    ppermute x4, waiting for transfers between devices, passed_along(): lax.ppermute(x, axis, [(i, (i + by) % length) for i in range(length)])  2.26 us
  transfers between devices with their start and end apart: 5, of which 2 were waited for; matrix products, arithmetic and copies ran while one was open for 14% of the time, Pallas kernels for 0%

commit v1 on v0

--- a/solution.py
+++ b/solution.py
@@ -4,6 +4,18 @@
 from jax.sharding import PartitionSpec as P
 
 REACH = 1
+
+
+def gather_by_bits(x, axis, dim):
+    ways, here = (lax.axis_size(axis), lax.axis_index(axis))
+    grown, reach = (x, 1)
+    while reach < ways:
+        theirs = lax.ppermute(grown, axis, [(d, d ^ reach) for d in range(ways)])
+        mine_first = jnp.concatenate([grown, theirs], axis=dim)
+        theirs_first = jnp.concatenate([theirs, grown], axis=dim)
+        grown = jnp.where(here & reach == 0, mine_first, theirs_first)
+        reach = 2 * reach
+    return grown
 
 
 def passed_along(x, axis, by):
@@ -41,7 +53,7 @@
     mine = lax.axis_index("grp")
     group_x, group_w = (
         lax.all_gather(unit_x, "grp", axis=0, tiled=True),
-        lax.all_gather(row_weight, "grp", axis=0, tiled=True),
+        gather_by_bits(row_weight, "grp", 0),
     )
     window = {0: unit_y}
     current = unit_y

time: 63.7 us -> 59.6 us (0.936)
  blocking collectives: 18.7 us -> 14.3 us
  starting transfers between devices: 8.24 us -> 11.1 us
  waiting for transfers between devices: 4.21 us -> 2.33 us
  local copies, waits for them, and re-layouts: 1.9 us -> 1.26 us
    all_gather x1 -> x0, blocking collectives: 4.22 us -> none  [shards(): lax.all_gather(row_weight, 'grp', axis=0, tiled=True)]
    reduce_scatter x1, waiting for transfers between devices: 1.94 us -> 0.05 us  [shards(): lax.psum_scatter(grad_group, 'grp', scatter_dimension=0, tiled=True)]
    ppermute x0 -> x1, starting transfers between devices: none -> 1.49 us  [gather_by_bits(): theirs = lax.ppermute(grown, axis, [(d, d ^ reach) for d in range(ways)])]
    ppermute x4, starting transfers between devices: 8.2 us -> 9.62 us  [passed_along(): lax.ppermute(x, axis, [(i, (i + by) % length) for i in range(length)])]
    unnamed x11, local copies, waits for them, and re-layouts: 1.9 us -> 1.26 us
  transfers between devices with their start and end apart: 5 -> 6, of which waited for: 2 -> 1; matrix products, arithmetic and copies ran while one was open for 14% -> 15% of each run, Pallas kernels for 0% -> 0%
where the time goes in v1:
time: 59.6 us; the launch traced here: 59.4 us
  between operations  16.2 us (27%)
  blocking collectives  14.3 us (24%)
  starting transfers between devices  11.1 us (19%)
  matrix products  9.11 us (15%)
  other arithmetic  5.09 us (9%)
  waiting for transfers between devices  2.33 us (4%)
  local copies, waits for them, and re-layouts  1.26 us (2%)
    ppermute x4, starting transfers between devices, passed_along(): lax.ppermute(x, axis, [(i, (i + by) % length) for i in range(length)])  9.62 us
    all_gather x1, blocking collectives, shards(): lax.all_gather(unit_x, 'grp', axis=0, tiled=True)  9.11 us
    unnamed x1, blocking collectives  5.14 us
    dot_general x3, matrix products, shards(): jnp.dot(slope, window[offset], precision=lax.Precision.HIGHEST)  3.46 us
    dot_general x3, matrix products, tile_terms(): jnp.einsum('id,jd->ij', left, right, precision=lax.Precision.HIGHEST)  3 us
    dot_general x3, matrix products, shards(): jnp.einsum('ij,id->jd', slope, group_x, precision=lax.Precision.HIGHEST)  2.65 us
    ppermute x4, waiting for transfers between devices, passed_along(): lax.ppermute(x, axis, [(i, (i + by) % length) for i in range(length)])  2.27 us
    mul x2, other arithmetic, unnormed(): return scale * (grad - unit * jnp.sum(unit * grad, axis=1, keepdims=True))  1.77 us
  transfers between devices with their start and end apart: 6, of which 1 were waited for; matrix products, arithmetic and copies ran while one was open for 15% of the time, Pallas kernels for 0%

profile of v1, /device:TPU:0, one launch (start us, length us, event | category | flops | bytes accessed | tf_op | source)
XLA Modules:
  0.0 59.4 jit_solution(1640335175316993740)
XLA Ops:
  7.2 1.1 %multiply_reduce_fusion.2 = f32[128]{0:T(128)S(1)} fusion(f32[128,768]{1,0:T(8,128)} %param.6), kind=kLoop, calls=%fused_computation.19 | loop fusion | flops 196480 | bytes 393728 | tf_op jit(solution)/shard_map/reduce_sum | solution.py:27
  8.5 5.5 %collective-permute-start.1 = (f32[128,768]{1,0:T(8,128)S(1)}, f32[128,768]{1,0:T(8,128)S(1)}, u32[]{:S(2)}, u32[]{:S(2)}) collective-permute-start(f32[128,768]{1,0:T(8,128)S(1)} %broadcast_multiply_fusion), channel_id=1, source_target_pairs={{0,30},{2,0},{4,2},{6,4},{8,6},{10,8},{12,10},{14,12},{16,14},{18,... | collective-permute-start | bytes 1179656 | tf_op jit(solution)/shard_map/ppermute | solution.py:23
  14.0 1.5 %collective-permute-start.2 = (f32[128]{0:T(128)S(1)}, f32[128]{0:T(128)S(1)}, u32[]{:S(2)}, u32[]{:S(2)}) collective-permute-start(f32[128]{0:T(128)S(1)} %copy-done.3), channel_id=1, source_target_pairs={{0,1},{1,0},{2,3},{3,2},{4,5},{5,4},{6,7},{7,6},{8,9},{9,8},{10,11... | collective-permute-start | bytes 1544 | tf_op jit(solution)/shard_map/ppermute | solution.py:13
  16.2 0.1 multiply_reduce_fusion.3
  16.3 0.1 broadcast_multiply_fusion.1
  16.4 9.1 %all_gather.3 = f32[256,768]{1,0:T(8,128)S(1)} all-gather(f32[128,768]{1,0:T(8,128)S(1)} %broadcast_multiply_fusion.1), channel_id=1, replica_groups=mesh['blk'=16,'grp'=2] {'grp'}, dimensions={0}, use_global_device_ids=true | all-gather | bytes 1179648 | tf_op jit(solution)/shard_map/all_gather | solution.py:55
  26.3 1.0 %fusion.9 = (f32[256]{0:T(256)S(1)}, f32[256,128]{0,1:T(8,128)S(1)}) fusion(f32[]{:T(128)} %bitcast.17, f32[256,768]{1,0:T(8,128)S(1)} %all_gather.3, f32[128,768]{1,0:T(8,128)S(1)} %broadcast_multiply_fusion, f32[]{:T(128)} %bitcast, s32[128]{0:T(128)S(1)} %iota_add_fusion), kind=kOutput, calls=%fused_computation.27 | convolution fusion | flops 302415616 | bytes 1312264 | tf_op jit(solution)/shard_map/id,jd->ij/dot_general | solution.py:37
  27.3 0.9 %fusion.16 = f32[256,768]{1,0:T(8,128)S(1)} fusion(f32[128,768]{1,0:T(8,128)S(1)} %broadcast_multiply_fusion, f32[256,128]{0,1:T(8,128)S(1)} %get-tuple-element.8, f32[256]{0:T(256)S(1)} %maximum_select_fusion, s32[128]{0:T(128)S(1)} %iota_add_fusion), kind=kOutput, calls=%fused_computation.45 | convolution fusion | flops 302252032 | bytes 1312256 | tf_op jit(solution)/shard_map/dot_general | solution.py:78
  28.2 1.0 %fusion.10 = (f32[256]{0:T(256)S(1)}, f32[256,128]{0,1:T(8,128)S(1)}) fusion(f32[]{:T(128)} %bitcast.16, f32[256,768]{1,0:T(8,128)S(1)} %all_gather.3, f32[128,768]{1,0:T(8,128)S(1)} %collective-permute-done.1, f32[]{:T(128)} %bitcast), kind=kOutput, calls=%fused_computation.28 | convolution fusion | flops 302284544 | bytes 1311752 | tf_op jit(solution)/shard_map/id,jd->ij/dot_general | solution.py:37
  29.2 0.8 %fusion.11 = f32[256,768]{1,0:T(8,128)S(1)} fusion(f32[128,768]{1,0:T(8,128)S(1)} %collective-permute-done.1, f32[256,128]{0,1:T(8,128)S(1)} %get-tuple-element.4, f32[256]{0:T(256)S(1)} %maximum_select_fusion), kind=kOutput, calls=%fused_computation.34 | convolution fusion | flops 302120960 | bytes 1311744 | tf_op jit(solution)/shard_map/dot_general | solution.py:78
  30.1 1.0 %fusion.8 = (f32[256]{0:T(256)S(1)}, f32[256,128]{0,1:T(8,128)S(1)}) fusion(f32[]{:T(128)} %bitcast.15, f32[256,768]{1,0:T(8,128)S(1)} %all_gather.3, f32[128,768]{1,0:T(8,128)S(1)} %collective-permute-done, f32[]{:T(128)} %bitcast), kind=kOutput, calls=%fused_computation.26 | convolution fusion | flops 302284544 | bytes 1311752 | tf_op jit(solution)/shard_map/id,jd->ij/dot_general | solution.py:37
  31.1 1.7 %fusion.1 = f32[256,768]{1,0:T(8,128)} fusion(f32[256,768]{1,0:T(8,128)S(1)} %fusion.11, f32[256,768]{1,0:T(8,128)S(1)} %fusion.16, f32[128,768]{1,0:T(8,128)S(1)} %collective-permute-done, f32[]{:T(128)} %bitcast, f32[256,128]{0,1:T(8,128)S(1)} %get-tuple-element.6, f32[256]{0:T(256)S(1)} %maximum_select_fusion), kind=kOutput, calls=%fused_computation.2 | convolution fusion | flops 302710784 | bytes 2884612 | tf_op jit(solution)/shard_map/dot_general | solution.py:78
  32.8 1.3 %convolution_multiply_fusion = f32[128,768]{1,0:T(8,128)} fusion(f32[256,768]{1,0:T(8,128)S(1)} %all_gather.3, f32[]{:T(128)} %bitcast, f32[256,128]{0,1:T(8,128)S(1)} %get-tuple-element.6, f32[256]{0:T(256)S(1)} %maximum_select_fusion), kind=kOutput, calls=%fused_computation.3 | convolution fusion | flops 302219264 | bytes 1311748 | tf_op jit(solution)/shard_map/ij,id->jd/dot_general | solution.py:81
  34.2 0.6 convolution_multiply_fusion.1
  34.8 4.1 %collective-permute-start.4 = (f32[128,768]{1,0:T(8,128)}, f32[128,768]{1,0:T(8,128)S(1)}, u32[]{:S(2)}, u32[]{:S(2)}) collective-permute-start(f32[128,768]{1,0:T(8,128)} %convolution_multiply_fusion), channel_id=1, source_target_pairs={{0,30},{2,0},{4,2},{6,4},{8,6},{10,8},{12,10},{14,12},{16,14},{18,... | collective-permute-start | bytes 1179656 | tf_op jit(solution)/shard_map/ppermute | solution.py:23
  38.8 0.7 %copy-done.4 = u32[32]{0:T(128)S(1)} copy-done((u32[32]{0:T(128)S(1)}, u32[32]{0:T(128)}, u32[]{:S(2)}) %copy-start.4) | copy-done | bytes 152
  39.5 0.6 dynamic-slice
  40.7 5.1 %all-reduce = f32[256]{0:T(256)S(1)} all-reduce(f32[256]{0:T(256)S(1)} %add_add_fusion), channel_id=2, replica_groups=mesh['blk'=16,'grp'=2] {'grp'}, use_global_device_ids=true, to_apply=%region_5.6.clone | all-reduce | flops 256 | bytes 2048
  45.9 0.6 dynamic-slice_multiply_fusion
  46.5 2.3 %collective-permute-done.3 = f32[128,768]{1,0:T(8,128)S(1)} collective-permute-done((f32[128,768]{1,0:T(8,128)S(1)}, f32[128,768]{1,0:T(8,128)S(1)}, u32[]{:S(2)}, u32[]{:S(2)}) %collective-permute-start.3) | collective-permute-done | bytes 393248 | tf_op jit(solution)/shard_map/ppermute | solution.py:23
  48.7 0.7 %multiply_reduce_fusion = (f32[128]{0:T(128)S(1)}, f32[128,768]{1,0:T(8,128)S(1)}) fusion(f32[128,768]{1,0:T(8,128)S(1)} %broadcast_multiply_fusion, f32[128,768]{1,0:T(8,128)S(1)} %collective-permute-done.4, f32[128,768]{1,0:T(8,128)S(1)} %collective-permute-done.3, f32[256,768]{1,0:T(8,128)S(1)} %all_gather.3, f32[256,128]{0,1:T(8,128)S(1)} %get-tuple-element.8, ...), kind=kOutput, calls=%fused_computation.16 | convolution fusion | flops 302743424 | bytes 2492420 | tf_op jit(solution)/shard_map/ij,id->jd/dot_general | solution.py:81
  49.5 0.9 %subtract_multiply_fusion = f32[128,768]{1,0:T(8,128)} fusion(f32[128,768]{1,0:T(8,128)S(1)} %get-tuple-element.10, f32[128]{0:T(128)S(1)} %get-tuple-element.9, f32[128]{0:T(128)S(1)} %add_rsqrt_fusion, f32[128,768]{1,0:T(8,128)S(1)} %copy-done.1), kind=kLoop, calls=%fused_computation.15 | loop fusion | flops 393216 | bytes 1180672 | tf_op jit(solution)/shard_map/mul | solution.py:32
  50.4 1.2 %multiply_reduce_fusion.1 = f32[128]{0:T(128)S(1)} fusion(f32[128,768]{1,0:T(8,128)} %reduce-scatter.2.cloned.1.call-done, f32[128,768]{1,0:T(8,128)S(1)} %copy-done, f32[128]{0:T(128)S(1)} %add_rsqrt_fusion.1), kind=kLoop, calls=%fused_computation.18 | loop fusion | flops 294784 | bytes 787456 | tf_op jit(solution)/shard_map/reduce_sum | solution.py:32
  51.7 0.9 %subtract_multiply_fusion.1 = f32[128,768]{1,0:T(8,128)} fusion(f32[128,768]{1,0:T(8,128)S(1)} %copy-done.2, f32[128]{0:T(128)S(1)} %multiply_reduce_fusion.1, f32[128]{0:T(128)S(1)} %add_rsqrt_fusion.1, f32[128,768]{1,0:T(8,128)S(1)} %copy-done), kind=kLoop, calls=%fused_computation.17 | loop fusion | flops 393216 | bytes 1180672 | tf_op jit(solution)/shard_map/mul | solution.py:32
  (24 shorter events, 0.3 us)
Async XLA Ops:
  7.2 1.2 %copy-start.1 = (f32[128,768]{1,0:T(8,128)S(1)}, f32[128,768]{1,0:T(8,128)}, u32[]{:S(2)}) copy-start(f32[128,768]{1,0:T(8,128)} %param.6) | copy-start | bytes 1179652
  7.2 43.2 %reduce-scatter.2.cloned.1.call-start = ((), (), s32[]{:S(2)}) async-start(), calls=%async_computation.1 | async-start | bytes 1179648 | tf_op jit(solution)/shard_map/reduce_scatter | solution.py:90
  8.4 5.7 %copy-start.3 = (f32[128]{0:T(128)S(1)}, f32[128]{0:T(128)}, u32[]{:S(2)}) copy-start(f32[128]{0:T(128)} %param.9) | copy-start | bytes 1540
  8.4 7.8 %copy-start = (f32[128,768]{1,0:T(8,128)S(1)}, f32[128,768]{1,0:T(8,128)}, u32[]{:S(2)}) copy-start(f32[128,768]{1,0:T(8,128)} %param.5) | copy-start | bytes 1179652
  8.5 19.7 %collective-permute-start.1 = (f32[128,768]{1,0:T(8,128)S(1)}, f32[128,768]{1,0:T(8,128)S(1)}, u32[]{:S(2)}, u32[]{:S(2)}) collective-permute-start(f32[128,768]{1,0:T(8,128)S(1)} %broadcast_multiply_fusion), channel_id=1, source_target_pairs={{0,30},{2,0},{4,2},{6,4},{8,6},{10,8},{12,10},{14,12},{16,14},{18,... | collective-permute-start | bytes 1179656 | tf_op jit(solution)/shard_map/ppermute | solution.py:23
  14.0 16.0 %collective-permute-start = (f32[128,768]{1,0:T(8,128)S(1)}, f32[128,768]{1,0:T(8,128)S(1)}, u32[]{:S(2)}, u32[]{:S(2)}) collective-permute-start(f32[128,768]{1,0:T(8,128)S(1)} %broadcast_multiply_fusion), channel_id=1, source_target_pairs={{0,2},{2,4},{4,6},{6,8},{8,10},{10,12},{12,14},{14,16},{16,18},{18... | collective-permute-start | bytes 1179656 | tf_op jit(solution)/shard_map/ppermute | solution.py:23
  14.0 13.2 %collective-permute-start.2 = (f32[128]{0:T(128)S(1)}, f32[128]{0:T(128)S(1)}, u32[]{:S(2)}, u32[]{:S(2)}) collective-permute-start(f32[128]{0:T(128)S(1)} %copy-done.3), channel_id=1, source_target_pairs={{0,1},{1,0},{2,3},{3,2},{4,5},{5,4},{6,7},{7,6},{8,9},{9,8},{10,11... | collective-permute-start | bytes 1544 | tf_op jit(solution)/shard_map/ppermute | solution.py:13
  34.8 11.7 %collective-permute-start.4 = (f32[128,768]{1,0:T(8,128)}, f32[128,768]{1,0:T(8,128)S(1)}, u32[]{:S(2)}, u32[]{:S(2)}) collective-permute-start(f32[128,768]{1,0:T(8,128)} %convolution_multiply_fusion), channel_id=1, source_target_pairs={{0,30},{2,0},{4,2},{6,4},{8,6},{10,8},{12,10},{14,12},{16,14},{18,... | collective-permute-start | bytes 1179656 | tf_op jit(solution)/shard_map/ppermute | solution.py:23
  38.8 9.9 %collective-permute-start.3 = (f32[128,768]{1,0:T(8,128)S(1)}, f32[128,768]{1,0:T(8,128)S(1)}, u32[]{:S(2)}, u32[]{:S(2)}) collective-permute-start(f32[128,768]{1,0:T(8,128)S(1)} %convolution_multiply_fusion.1), channel_id=1, source_target_pairs={{0,2},{2,4},{4,6},{6,8},{8,10},{10,12},{12,14},{14,16},{16,18},{18... | collective-permute-start | bytes 1179656 | tf_op jit(solution)/shard_map/ppermute | solution.py:23
  38.8 0.7 %copy-start.4 = (u32[32]{0:T(128)S(1)}, u32[32]{0:T(128)}, u32[]{:S(2)}) copy-start(u32[32]{0:T(128)} %constant.30) | copy-start | bytes 388
  50.4 1.3 %copy-start.2 = (f32[128,768]{1,0:T(8,128)S(1)}, f32[128,768]{1,0:T(8,128)}, u32[]{:S(2)}) copy-start(f32[128,768]{1,0:T(8,128)} %reduce-scatter.2.cloned.1.call-done) | copy-start | bytes 1179652
Sparse Core Ops, SparseCore 0:
  32.9 17.4 reduce-scatter.1
